TPU v7x, 256 devices: a whole 4x4x8 slice. The times are simulated.
256 devices in a mesh: section: 2 (over core), row: 32 (over z, y), col: 4 (over x).
Axes of the slice: x: 4, y: 4, z: 8, core: 2. Of those that a mesh axis runs over, the one named last changes fastest.
Arguments:
- hidden_in: bfloat16 [32, 256, 3072], P('row', None, 'col')
- patch_ends: int32 [32, 4], P('row'), may hold values from 1 to 256, as said below
- timestep: int32 [32], P('row'), may hold values from 0 to 999
- mod_weight: bfloat16 [2, 256, 3, 3072], P('section'), may hold values from -0.75 to 0.75
- qkv_weight: bfloat16 [2, 3072, 3, 3072], P('section', 'row', None, 'col'), may hold values from -0.109375 to 0.109375
- out_weight: bfloat16 [2, 3072, 3072], P('section', 'col', 'row'), may hold values from -0.109375 to 0.109375
- stale_keys: bfloat16 [2, 32, 256, 3072], P('section', 'row', None, 'col'), may hold values from -1.5 to 1.5
- stale_values: bfloat16 [2, 32, 256, 3072], P('section', 'row', None, 'col'), may hold values from -6 to 6
Outputs:
- layer_out: bfloat16 [2, 32, 256, 3072], P('section', 'row', None, 'col')
Inputs may be any that keep to these rules, and one draw needn't show every extreme that they name: patch_ends rises along each request's 4 patches; each patch holds at least one and at most 64 positions, and in every draw some request has all 4 patches of exactly 64 positions.
All inputs are finite; a program needn't handle non-finite values.
Results may differ from a plain program's by a relative error of at most 0.018.
Values may be sent and summed in bfloat16 or wider, within the bound.
A program may use at most 128 MiB of HBM per device.

v0:
```python
import math
import jax
import jax.numpy as jnp
from jax import lax
from jax.sharding import PartitionSpec as P

HD = 128
FREQ = 256
NP = 4
PATCH = 64


def passed_along(array, axis, by):
    length = lax.axis_size(axis)
    pairs = [(i, i + by) for i in range(length) if 0 <= i + by < length]
    return lax.ppermute(array, axis, pairs)


def embed_time(timestep, feat_width):
    half_width = feat_width // 2
    frequency = jnp.exp(
        jnp.arange(half_width, dtype=jnp.float32) * (-math.log(10000.0) / half_width)
    )
    angles = timestep.astype(jnp.float32)[:, None] * frequency[None, :]
    return jnp.concatenate([jnp.cos(angles), jnp.sin(angles)], axis=1).astype(jnp.bfloat16)


def head_norm(raw_proj):
    shaped = raw_proj.reshape(raw_proj.shape[:-1] + (raw_proj.shape[-1] // HD, HD))
    scaled = shaped / jnp.sqrt(jnp.mean(shaped * shaped, axis=-1, keepdims=True) + 1e-06)
    return scaled.reshape(raw_proj.shape).astype(jnp.bfloat16)


def slice_one(source, first_row):
    return lax.dynamic_slice_in_dim(source, first_row, PATCH, 0)


def update_one(source, new_rows, first_row):
    return lax.dynamic_update_slice_in_dim(source, new_rows, first_row, 0)


def take_rows(source, row_begin):
    return jax.vmap(slice_one)(source, row_begin)


def put_rows(source, new_rows, row_begin, row_count, is_active):
    previous = take_rows(source, row_begin)
    keep_new = (jnp.arange(PATCH)[None, :, None] < row_count[:, None, None]) & is_active
    merged = jnp.where(keep_new, new_rows, previous)
    return jax.vmap(update_one)(source, merged, row_begin)


def attend_rows(queries, key_rows, value_rows, key_ok):
    requests = queries.shape[0]
    query_heads = queries.reshape(requests, queries.shape[1], -1, HD)
    key_heads = key_rows.reshape(requests, key_rows.shape[1], -1, HD)
    value_heads = value_rows.reshape(requests, value_rows.shape[1], -1, HD)
    scores = jnp.einsum(
        "bqhd,bkhd->bhqk", query_heads, key_heads, preferred_element_type=jnp.float32
    ) / math.sqrt(HD)
    weights = jnp.exp(scores) * key_ok[:, None, None, :]
    weights = (weights / jnp.sum(weights, axis=-1, keepdims=True)).astype(jnp.bfloat16)
    mixed = jnp.einsum("bhqk,bkhd->bqhd", weights, value_heads, preferred_element_type=jnp.float32)
    return mixed.reshape(queries.shape).astype(jnp.bfloat16)


def modulated_rows(patch_rows, shift_vec, scale_vec, col_index, col_width):
    feat_width = shift_vec.shape[-1]
    as_float = patch_rows.astype(jnp.float32)
    sum_rows, sum_squares = lax.psum(
        (jnp.sum(as_float, axis=-1), jnp.sum(as_float * as_float, axis=-1)), "col"
    )
    row_mean = (sum_rows / feat_width)[:, :, None]
    row_var = (sum_squares / feat_width)[:, :, None] - row_mean * row_mean
    shift_own = lax.dynamic_slice_in_dim(shift_vec, col_index * col_width, col_width, 1)
    scale_own = lax.dynamic_slice_in_dim(scale_vec, col_index * col_width, col_width, 1)
    normed = (as_float - row_mean) / jnp.sqrt(row_var + 1e-06)
    local_rows = (normed * (1.0 + scale_own[:, None, :]) + shift_own[:, None, :]).astype(
        jnp.bfloat16
    )
    return lax.all_gather(local_rows, "col", axis=2, tiled=True)


def shards(
    hidden_in, patch_ends, timestep, mod_weight, qkv_weight, out_weight, stale_keys, stale_values
):
    section_index = lax.axis_index("section")
    col_index = lax.axis_index("col")
    requests, slot_len, col_width = hidden_in.shape
    feat_width = mod_weight.shape[-1]
    qkv_full = lax.all_gather(qkv_weight, "row", axis=1, tiled=True)
    out_full = lax.all_gather(out_weight, "row", axis=2, tiled=True)
    qkv_matrix = qkv_full[0].reshape(feat_width, 3 * col_width)
    out_matrix = out_full[0]
    time_feats = embed_time(timestep, FREQ)
    modulation = jnp.dot(
        time_feats, mod_weight[0].reshape(FREQ, 3 * feat_width), preferred_element_type=jnp.float32
    ).reshape(requests, 3, feat_width)
    shift_vec = modulation[:, 0]
    scale_vec = modulation[:, 1]
    gate_own = lax.dynamic_slice_in_dim(modulation[:, 2], col_index * col_width, col_width, 1)
    padding = jnp.zeros((requests, PATCH, col_width), jnp.bfloat16)
    input_pad = jnp.concatenate([hidden_in, padding], axis=1)
    key_cache = jnp.concatenate([stale_keys[0], padding], axis=1)
    value_cache = jnp.concatenate([stale_values[0], padding], axis=1)
    result_pad = jnp.zeros((requests, slot_len + PATCH, col_width), jnp.bfloat16)
    patch_starts = jnp.concatenate(
        [jnp.zeros((requests, 1), jnp.int32), patch_ends[:, : NP - 1]], axis=1
    )
    seq_len = patch_ends[:, NP - 1]
    key_ok = (jnp.arange(slot_len)[None, :] < seq_len[:, None]).astype(jnp.float32)
    row_ids = jnp.arange(PATCH)
    received = padding
    for step_index in range(NP + 1):
        offset = step_index - section_index
        is_active = (offset >= 0) & (offset < NP)
        patch_index = jnp.clip(offset, 0, NP - 1)
        row_begin = jnp.take(patch_starts, patch_index, axis=1)
        row_count = jnp.take(patch_ends, patch_index, axis=1) - row_begin
        patch_rows = jnp.where(section_index == 0, take_rows(input_pad, row_begin), received)
        modulated = modulated_rows(patch_rows, shift_vec, scale_vec, col_index, col_width)
        projected = jnp.dot(
            modulated.reshape(-1, feat_width), qkv_matrix, preferred_element_type=jnp.float32
        ).reshape(requests, PATCH, 3, col_width)
        queries = head_norm(projected[:, :, 0])
        key_cache = put_rows(
            key_cache, head_norm(projected[:, :, 1]), row_begin, row_count, is_active
        )
        value_cache = put_rows(
            value_cache, projected[:, :, 2].astype(jnp.bfloat16), row_begin, row_count, is_active
        )
        attended = attend_rows(queries, key_cache[:, :slot_len], value_cache[:, :slot_len], key_ok)
        partial_out = jnp.dot(
            attended.reshape(-1, col_width), out_matrix, preferred_element_type=jnp.float32
        ).reshape(requests, PATCH, feat_width)
        summed = lax.psum_scatter(
            partial_out.astype(jnp.bfloat16), "col", scatter_dimension=2, tiled=True
        ).astype(jnp.float32)
        updated = patch_rows.astype(jnp.float32) + gate_own[:, None, :] * summed
        within = row_ids[None, :, None] < row_count[:, None, None]
        new_rows = jnp.where(within, updated, 0.0).astype(jnp.bfloat16)
        result_pad = put_rows(result_pad, new_rows, row_begin, row_count, is_active)
        if step_index < NP:
            received = passed_along(new_rows, "section", 1)
    return result_pad[None, :, :slot_len]


def solution(mesh):
    return jax.shard_map(
        shards,
        mesh=mesh,
        in_specs=(
            P("row", None, "col"),
            P("row", None),
            P("row"),
            P("section", None, None, None),
            P("section", "row", None, "col"),
            P("section", "col", "row"),
            P("section", "row", None, "col"),
            P("section", "row", None, "col"),
        ),
        out_specs=P("section", "row", None, "col"),
        check_vma=False,
    )
```

profile of v0, /device:TPU:8, one launch (start us, length us, event | category | flops | bytes accessed | tf_op | source)
XLA Modules:
  0.0 542.1 jit_solution(13146894626585429524)
XLA Ops:
  8.8 1.6 constant_dynamic-slice_fusion.8
  17.1 6.7 %copy.135 = bf16[1,256,3,3072]{1,3,2,0:T(8,128)(2,1)} copy(bf16[1,256,3,3072]{3,1,2,0:T(8,128)(2,1)} %param.41) | data formatting | bytes 9437184 | tf_op args[3]
  23.9 10.5 %all-reduce.7 = (f32[1,64]{1,0:T(1,128)S(1)}, f32[1,64]{1,0:T(1,128)S(1)}) all-reduce(f32[1,64]{1,0:T(1,128)S(1)} %bitcast.463, f32[1,64]{1,0:T(1,128)S(1)} %bitcast.462), channel_id=1, replica_groups=mesh['section'=2,'row'=32,'col'=4] {'col'}, use_global_device_ids=true, to_apply=%region_4.5 | all-reduce | flops 128 | bytes 1024 | tf_op jit(solution)/shard_map/psum | solution.py:70
  34.4 3.7 fusion.10
  40.9 4.6 and_reduce_fusion
  45.6 12.5 %all_gather.21 = bf16[1,64,3072]{2,1,0:T(8,128)(2,1)S(1)} all-gather(bf16[1,64,768]{2,1,0:T(8,128)(2,1)S(1)} %fusion.90), channel_id=1, replica_groups=mesh['section'=2,'row'=32,'col'=4] {'col'}, dimensions={2}, use_global_device_ids=true | all-gather | bytes 491520 | tf_op jit(solution)/shard_map/all_gather | solution.py:81
  58.1 81.0 %all-gather.3.cloned.1.call-done = bf16[1,3072,3,768]{3,1,2,0:T(8,128)(2,1)} async-done(((bf16[1,96,3,768]{3,1,2,0:T(8,128)(2,1)}), bf16[1,3072,3,768]{3,1,2,0:T(8,128)(2,1)}) %all-gather.3.cloned.1.call-update) | async-done | bytes 14155792 | tf_op jit(solution)/shard_map/all_gather | solution.py:91
  139.1 18.7 %copy.136 = bf16[1,3072,3,768]{1,3,2,0:T(8,128)(2,1)} copy(bf16[1,3072,3,768]{3,1,2,0:T(8,128)(2,1)} %all-gather.3.cloned.1.call-done) | data formatting | bytes 28311552 | tf_op jit(solution)/shard_map/all_gather | solution.py:91
  157.8 9.5 %fusion.52 = f32[1,64,3,768]{3,1,2,0:T(8,128)S(1)} fusion(bf16[1,3072,3,768]{1,3,2,0:T(8,128)(2,1)} %copy.136, bf16[1,64,3072]{2,1,0:T(8,128)(2,1)S(1)} %all_gather.21), kind=kOutput, calls=%fused_computation.32 | convolution fusion | flops 905969664 | bytes 15138816 | tf_op jit(solution)/shard_map/dot_general | solution.py:122
  175.3 47.0 %all-gather.5.cloned.1.call-done = bf16[1,768,3072]{1,2,0:T(8,128)(2,1)} async-done(((bf16[1,768,96]{1,2,0:T(8,128)(2,1)}), bf16[1,768,3072]{1,2,0:T(8,128)(2,1)}) %all-gather.5.cloned.1.call-update) | async-done | bytes 4718608 | tf_op jit(solution)/shard_map/all_gather | solution.py:92
  222.4 4.6 fusion.49
  229.0 3.3 and_reduce_fusion.2
  232.3 16.8 %reduce-scatter.6.cloned.1.call-done = bf16[1,64,768]{2,1,0:T(8,128)(2,1)} async-done(((bf16[1,64,3072]{2,1,0:T(8,128)(2,1)}), bf16[1,64,768]{2,1,0:T(8,128)(2,1)}) %reduce-scatter.6.cloned.1.call-update) | async-done | bytes 98320 | tf_op jit(solution)/shard_map/reduce_scatter | solution.py:136
  249.0 1.6 select_select_fusion
  253.0 8.6 %all-reduce.6 = (f32[1,64]{1,0:T(1,128)S(1)}, f32[1,64]{1,0:T(1,128)S(1)}) all-reduce(f32[1,64]{1,0:T(1,128)S(1)} %bitcast.457, f32[1,64]{1,0:T(1,128)S(1)} %bitcast.456), channel_id=1, replica_groups=mesh['section'=2,'row'=32,'col'=4] {'col'}, use_global_device_ids=true, to_apply=%region_13.14 | all-reduce | flops 128 | bytes 1024 | tf_op jit(solution)/shard_map/psum | solution.py:70
  261.8 12.9 %all_gather.24 = bf16[1,64,3072]{2,1,0:T(8,128)(2,1)S(1)} all-gather(bf16[1,64,768]{2,1,0:T(8,128)(2,1)S(1)} %fusion.97), channel_id=1, replica_groups=mesh['section'=2,'row'=32,'col'=4] {'col'}, dimensions={2}, use_global_device_ids=true | all-gather | bytes 491520 | tf_op jit(solution)/shard_map/all_gather | solution.py:81
  274.6 9.4 %fusion.55 = f32[1,64,3,768]{3,1,2,0:T(8,128)S(1)} fusion(bf16[1,3072,3,768]{1,3,2,0:T(8,128)(2,1)} %copy.136, bf16[1,64,3072]{2,1,0:T(8,128)(2,1)S(1)} %all_gather.24), kind=kOutput, calls=%fused_computation.33 | convolution fusion | flops 905969664 | bytes 15138816 | tf_op jit(solution)/shard_map/dot_general | solution.py:122
  290.7 4.6 fusion.46
  297.4 21.2 %reduce-scatter.8.cloned.1.call-done = bf16[1,64,768]{2,1,0:T(8,128)(2,1)} async-done(((bf16[1,64,3072]{2,1,0:T(8,128)(2,1)}), bf16[1,64,768]{2,1,0:T(8,128)(2,1)}) %reduce-scatter.8.cloned.1.call-update) | async-done | bytes 98320 | tf_op jit(solution)/shard_map/reduce_scatter | solution.py:136
  318.7 2.3 fusion.186
  323.4 8.6 %all-reduce.5 = (f32[1,64]{1,0:T(1,128)S(1)}, f32[1,64]{1,0:T(1,128)S(1)}) all-reduce(f32[1,64]{1,0:T(1,128)S(1)} %bitcast.459, f32[1,64]{1,0:T(1,128)S(1)} %bitcast.458), channel_id=1, replica_groups=mesh['section'=2,'row'=32,'col'=4] {'col'}, use_global_device_ids=true, to_apply=%region_22.23 | all-reduce | flops 128 | bytes 1024 | tf_op jit(solution)/shard_map/psum | solution.py:70
  332.1 12.7 %all_gather.25 = bf16[1,64,3072]{2,1,0:T(8,128)(2,1)S(1)} all-gather(bf16[1,64,768]{2,1,0:T(8,128)(2,1)S(1)} %fusion.104), channel_id=1, replica_groups=mesh['section'=2,'row'=32,'col'=4] {'col'}, dimensions={2}, use_global_device_ids=true | all-gather | bytes 491520 | tf_op jit(solution)/shard_map/all_gather | solution.py:81
  344.8 9.4 %fusion.58 = f32[1,64,3,768]{3,1,2,0:T(8,128)S(1)} fusion(bf16[1,3072,3,768]{1,3,2,0:T(8,128)(2,1)} %copy.136, bf16[1,64,3072]{2,1,0:T(8,128)(2,1)S(1)} %all_gather.25), kind=kOutput, calls=%fused_computation.34 | convolution fusion | flops 905969664 | bytes 15138816 | tf_op jit(solution)/shard_map/dot_general | solution.py:122
  355.2 2.0 fusion.142
  361.4 4.6 fusion.43
  368.2 21.1 %reduce-scatter.10.cloned.1.call-done = bf16[1,64,768]{2,1,0:T(8,128)(2,1)} async-done(((bf16[1,64,3072]{2,1,0:T(8,128)(2,1)}), bf16[1,64,768]{2,1,0:T(8,128)(2,1)}) %reduce-scatter.10.cloned.1.call-update) | async-done | bytes 98320 | tf_op jit(solution)/shard_map/reduce_scatter | solution.py:136
  389.3 2.3 fusion.185
  391.6 1.5 collective-permute-start.2
  394.0 8.6 %all-reduce.4 = (f32[1,64]{1,0:T(1,128)S(1)}, f32[1,64]{1,0:T(1,128)S(1)}) all-reduce(f32[1,64]{1,0:T(1,128)S(1)} %bitcast.461, f32[1,64]{1,0:T(1,128)S(1)} %bitcast.460), channel_id=1, replica_groups=mesh['section'=2,'row'=32,'col'=4] {'col'}, use_global_device_ids=true, to_apply=%region_31.32 | all-reduce | flops 128 | bytes 1024 | tf_op jit(solution)/shard_map/psum | solution.py:70
  402.8 12.6 %all_gather.26 = bf16[1,64,3072]{2,1,0:T(8,128)(2,1)S(1)} all-gather(bf16[1,64,768]{2,1,0:T(8,128)(2,1)S(1)} %fusion.111), channel_id=1, replica_groups=mesh['section'=2,'row'=32,'col'=4] {'col'}, dimensions={2}, use_global_device_ids=true | all-gather | bytes 491520 | tf_op jit(solution)/shard_map/all_gather | solution.py:81
  415.4 9.4 %fusion.61 = f32[1,64,3,768]{3,1,2,0:T(8,128)S(1)} fusion(bf16[1,3072,3,768]{1,3,2,0:T(8,128)(2,1)} %copy.136, bf16[1,64,3072]{2,1,0:T(8,128)(2,1)S(1)} %all_gather.26), kind=kOutput, calls=%fused_computation.35 | convolution fusion | flops 905969664 | bytes 15138816 | tf_op jit(solution)/shard_map/dot_general | solution.py:122
  425.8 2.0 fusion.144
  427.8 1.5 scatter.66
  429.3 1.5 scatter.65
  432.0 4.6 fusion.40
  438.8 21.3 %reduce-scatter.12.cloned.1.call-done = bf16[1,64,768]{2,1,0:T(8,128)(2,1)} async-done(((bf16[1,64,3072]{2,1,0:T(8,128)(2,1)}), bf16[1,64,768]{2,1,0:T(8,128)(2,1)}) %reduce-scatter.12.cloned.1.call-update) | async-done | bytes 98320 | tf_op jit(solution)/shard_map/reduce_scatter | solution.py:136
  460.1 2.3 fusion.184
  464.7 8.6 %all-reduce.3 = (f32[1,64]{1,0:T(1,128)S(1)}, f32[1,64]{1,0:T(1,128)S(1)}) all-reduce(f32[1,64]{1,0:T(1,128)S(1)} %bitcast.455, f32[1,64]{1,0:T(1,128)S(1)} %bitcast.454), channel_id=1, replica_groups=mesh['section'=2,'row'=32,'col'=4] {'col'}, use_global_device_ids=true, to_apply=%region_40.41 | all-reduce | flops 128 | bytes 1024 | tf_op jit(solution)/shard_map/psum | solution.py:70
  473.4 13.0 %all_gather.27 = bf16[1,64,3072]{2,1,0:T(8,128)(2,1)S(1)} all-gather(bf16[1,64,768]{2,1,0:T(8,128)(2,1)S(1)} %fusion.118), channel_id=1, replica_groups=mesh['section'=2,'row'=32,'col'=4] {'col'}, dimensions={2}, use_global_device_ids=true | all-gather | bytes 491520 | tf_op jit(solution)/shard_map/all_gather | solution.py:81
  486.4 9.4 %fusion.64 = f32[1,64,3,768]{3,1,2,0:T(8,128)S(1)} fusion(bf16[1,3072,3,768]{1,3,2,0:T(8,128)(2,1)} %copy.136, bf16[1,64,3072]{2,1,0:T(8,128)(2,1)S(1)} %all_gather.27), kind=kOutput, calls=%fused_computation.36 | convolution fusion | flops 905969664 | bytes 15138816 | tf_op jit(solution)/shard_map/dot_general | solution.py:122
  496.8 1.5 fusion.146
  498.3 1.5 scatter.71
  500.1 1.5 scatter.70
  502.7 4.6 fusion.37
  507.3 1.5 scatter.69
  508.8 21.8 %reduce-scatter.14.cloned.1.call-done = bf16[1,64,768]{2,1,0:T(8,128)(2,1)} async-done(((bf16[1,64,3072]{2,1,0:T(8,128)(2,1)}), bf16[1,64,768]{2,1,0:T(8,128)(2,1)}) %reduce-scatter.14.cloned.1.call-update) | async-done | bytes 98320 | tf_op jit(solution)/shard_map/reduce_scatter | solution.py:136
  530.6 2.4 fusion.163
  533.0 1.5 scatter.74
  (206 shorter events, 46.4 us)
Async XLA Ops:
  6.5 132.6 %all-gather.3.cloned.1.call-start = ((), (), s32[]{:S(2)}) async-start(), calls=%async_computation.5 | async-start | bytes 14598144 | tf_op jit(solution)/shard_map/all_gather | solution.py:91
  7.3 215.1 %all-gather.5.cloned.1.call-start = ((), (), s32[]{:S(2)}) async-start(), calls=%async_computation.6 | async-start | bytes 4866048 | tf_op jit(solution)/shard_map/all_gather | solution.py:92
  8.0 241.0 %reduce-scatter.6.cloned.1.call-start = ((), (), s32[]{:S(2)}) async-start(), calls=%async_computation.7 | async-start | bytes 491520 | tf_op jit(solution)/shard_map/reduce_scatter | solution.py:136
  17.1 6.7 %copy-start = (bf16[1,256,768]{2,1,0:T(8,128)(2,1)S(1)}, bf16[1,256,768]{2,1,0:T(8,128)(2,1)}, u32[]{:S(2)}) copy-start(bf16[1,256,768]{2,1,0:T(8,128)(2,1)} %param.38) | copy-start | bytes 1179652
  23.8 15.1 %copy-start.3 = (s32[1,2]{1,0:T(1,128)S(1)}, s32[1,2]{1,0:T(1,128)}, u32[]{:S(2)}) copy-start(s32[1,2]{1,0:T(1,128)} %constant.478.clone.1) | copy-start | bytes 28
  23.8 17.1 %copy-start.4 = (s32[3]{0:T(128)S(1)}, s32[3]{0:T(128)}, u32[]{:S(2)}) copy-start(s32[3]{0:T(128)} %constant.479.clone.1) | copy-start | bytes 40
  157.8 12.2 %copy-start.1 = (bf16[1,1,256,768]{3,2,1,0:T(8,128)(2,1)S(1)}, bf16[1,1,256,768]{3,2,1,0:T(8,128)(2,1)}, u32[]{:S(2)}) copy-start(bf16[1,1,256,768]{3,2,1,0:T(8,128)(2,1)} %param.45) | copy-start | bytes 1179652
  157.8 12.2 %copy-start.2 = (bf16[1,1,256,768]{3,2,1,0:T(8,128)(2,1)S(1)}, bf16[1,1,256,768]{3,2,1,0:T(8,128)(2,1)}, u32[]{:S(2)}) copy-start(bf16[1,1,256,768]{3,2,1,0:T(8,128)(2,1)} %param.44) | copy-start | bytes 1179652
  227.0 91.6 %reduce-scatter.8.cloned.1.call-start = ((), (), s32[]{:S(2)}) async-start(), calls=%async_computation.8 | async-start | bytes 491520 | tf_op jit(solution)/shard_map/reduce_scatter | solution.py:136
  250.6 2.2 collective-permute-start
  295.3 94.0 %reduce-scatter.10.cloned.1.call-start = ((), (), s32[]{:S(2)}) async-start(), calls=%async_computation.9 | async-start | bytes 491520 | tf_op jit(solution)/shard_map/reduce_scatter | solution.py:136
  321.0 2.2 collective-permute-start.1
  360.8 28.5 %copy-start.6 = (pred[64]{0:T(512)(128)(4,1)S(1)}, pred[64]{0:T(512)(128)(4,1)}, u32[]{:S(2)}) copy-start(pred[64]{0:T(512)(128)(4,1)} %broadcast_and_fusion.2) | copy-start | bytes 196
  366.0 94.0 %reduce-scatter.12.cloned.1.call-start = ((), (), s32[]{:S(2)}) async-start(), calls=%async_computation.10 | async-start | bytes 491520 | tf_op jit(solution)/shard_map/reduce_scatter | solution.py:136
  391.6 2.2 collective-permute-start.2
  431.4 28.6 %copy-start.5 = (pred[64]{0:T(512)(128)(4,1)S(1)}, pred[64]{0:T(512)(128)(4,1)}, u32[]{:S(2)}) copy-start(pred[64]{0:T(512)(128)(4,1)} %broadcast_and_fusion.1) | copy-start | bytes 196
  436.7 93.9 %reduce-scatter.14.cloned.1.call-start = ((), (), s32[]{:S(2)}) async-start(), calls=%async_computation.11 | async-start | bytes 491520 | tf_op jit(solution)/shard_map/reduce_scatter | solution.py:136
  462.3 2.2 collective-permute-start.3
Sparse Core Ops, SparseCore 0:
  9.9 129.1 all-gather.2
  141.7 80.6 all-gather.4
  227.1 21.8 reduce-scatter.5
  295.5 23.1 reduce-scatter.7
  366.2 23.0 reduce-scatter.9
  436.8 23.2 reduce-scatter.11
  507.4 23.0 reduce-scatter.13
where the time goes:
time: 544 us; the launch traced here: 542 us
  waiting for transfers between devices  234 us (43%)
  blocking collectives  109 us (20%)
  matrix products  76.5 us (14%)
  local copies, waits for them, and re-layouts  61.6 us (11%)
  other arithmetic  34.5 us (6%)
  between operations  21.4 us (4%)
  starting transfers between devices  5.65 us (1%)
    reduce_scatter x5, waiting for transfers between devices, shards(): lax.psum_scatter(partial_out.astype(jnp.bfloat16), 'col', scatter_dimensi...  102 us
    all_gather x1, waiting for transfers between devices, shards(): qkv_full = lax.all_gather(qkv_weight, 'row', axis=1, tiled=True)  81 us
    all_gather x5, blocking collectives, modulated_rows(): return lax.all_gather(local_rows, 'col', axis=2, tiled=True)  63.6 us
    dot_general x5, matrix products, shards(): jnp.dot(modulated.reshape(-1, feat_width), qkv_matrix, preferred_element_...  47.1 us
    all_gather x1, waiting for transfers between devices, shards(): out_full = lax.all_gather(out_weight, 'row', axis=2, tiled=True)  47 us
    psum x5, blocking collectives, modulated_rows(): lax.psum((jnp.sum(as_float, axis=-1), jnp.sum(as_float * as_float, axis=-...  44.9 us
    another operation x13, other arithmetic  27.1 us
    dot_general x5, matrix products, shards(): jnp.dot(attended.reshape(-1, col_width), out_matrix, preferred_element_ty...  23.1 us
  transfers between devices with their start and end apart: 11, of which 11 were waited for; matrix products, arithmetic and copies ran while one was open for 13% of the time, Pallas kernels for 0%

commit v1 on v0

--- a/solution.py
+++ b/solution.py
@@ -89,7 +89,9 @@
     requests, slot_len, col_width = hidden_in.shape
     feat_width = mod_weight.shape[-1]
     qkv_full = lax.all_gather(qkv_weight, "row", axis=1, tiled=True)
-    out_full = lax.all_gather(out_weight, "row", axis=2, tiled=True)
+    out_full = jnp.concatenate(
+        lax.all_to_all(jnp.stack([out_weight] * lax.axis_size("row")), "row", 0, 0), axis=2
+    )
     qkv_matrix = qkv_full[0].reshape(feat_width, 3 * col_width)
     out_matrix = out_full[0]
     time_feats = embed_time(timestep, FREQ)

time: 544 us -> 568 us (1.044)
  waiting for transfers between devices: 234 us -> 247 us
  starting transfers between devices: 5.65 us -> 17.5 us
    all_gather x1, waiting for transfers between devices: 81 us -> 141 us  [shards(): qkv_full = lax.all_gather(qkv_weight, 'row', axis=1, tiled=True)]
    all_gather x1 -> x0, waiting for transfers between devices: 47 us -> none  [shards(): out_full = lax.all_gather(out_weight, 'row', axis=2, tiled=True)]
    all_to_all x0 -> x1, starting transfers between devices: none -> 11.9 us  [shards(): lax.all_to_all(jnp.stack([out_weight] * lax.axis_size('row')), 'row', 0, 0)]
  transfers between devices with their start and end apart: 11 -> 11, of which waited for: 11 -> 10; matrix products, arithmetic and copies ran while one was open for 13% -> 12% of each run, Pallas kernels for 0% -> 0%
where the time goes in v1:
time: 568 us; the launch traced here: 566 us
  waiting for transfers between devices  247 us (43%)
  blocking collectives  109 us (19%)
  matrix products  76.3 us (13%)
  local copies, waits for them, and re-layouts  62.3 us (11%)
  other arithmetic  33.5 us (6%)
  between operations  21.7 us (4%)
  starting transfers between devices  17.5 us (3%)
    all_gather x1, waiting for transfers between devices, shards(): qkv_full = lax.all_gather(qkv_weight, 'row', axis=1, tiled=True)  141 us
    reduce_scatter x5, waiting for transfers between devices, shards(): lax.psum_scatter(partial_out.astype(jnp.bfloat16), 'col', scatter_dimensi...  102 us
    all_gather x5, blocking collectives, modulated_rows(): return lax.all_gather(local_rows, 'col', axis=2, tiled=True)  63.6 us
    dot_general x5, matrix products, shards(): jnp.dot(modulated.reshape(-1, feat_width), qkv_matrix, preferred_element_...  47 us
    psum x5, blocking collectives, modulated_rows(): lax.psum((jnp.sum(as_float, axis=-1), jnp.sum(as_float * as_float, axis=-...  44.9 us
    another operation x13, other arithmetic  26.8 us
    dot_general x5, matrix products, shards(): jnp.dot(attended.reshape(-1, col_width), out_matrix, preferred_element_ty...  23.1 us
    scatter x15, local copies, waits for them, and re-layouts, update_one(): return lax.dynamic_update_slice_in_dim(source, new_rows, first_row, 0)  22.2 us
  transfers between devices with their start and end apart: 11, of which 10 were waited for; matrix products, arithmetic and copies ran while one was open for 12% of the time, Pallas kernels for 0%

profile of v1, /device:TPU:8, one launch (start us, length us, event | category | flops | bytes accessed | tf_op | source)
XLA Modules:
  0.0 566.4 jit_solution(9769458300822851451)
XLA Ops:
  7.3 3.6 stack.2
  10.9 11.9 %all-to-all-start = ((bf16[32,1,768,96]{2,3,1,0:T(8,128)(2,1)}), bf16[32,1,768,96]{2,3,1,0:T(8,128)(2,1)}, u32[]{:S(2)}, u32[]{:S(2)}) async-start(bf16[32,1,768,96]{2,3,1,0:T(8,128)(2,1)} %stack.2), calls=%async_computation | async-start | bytes 9437184 | tf_op jit(solution)/shard_map/all_to_all | solution.py:93
  28.4 6.7 %copy.138 = bf16[1,256,3,3072]{1,3,2,0:T(8,128)(2,1)} copy(bf16[1,256,3,3072]{3,1,2,0:T(8,128)(2,1)} %param.41) | data formatting | bytes 9437184 | tf_op args[3]
  35.2 10.5 %all-reduce.7 = (f32[1,64]{1,0:T(1,128)S(1)}, f32[1,64]{1,0:T(1,128)S(1)}) all-reduce(f32[1,64]{1,0:T(1,128)S(1)} %bitcast.444, f32[1,64]{1,0:T(1,128)S(1)} %bitcast.443), channel_id=1, replica_groups=mesh['section'=2,'row'=32,'col'=4] {'col'}, use_global_device_ids=true, to_apply=%region_4.5 | all-reduce | flops 128 | bytes 1024 | tf_op jit(solution)/shard_map/psum | solution.py:70
  45.7 3.7 fusion.10
  52.1 4.5 and_reduce_fusion
  56.8 12.5 %all_gather.18 = bf16[1,64,3072]{2,1,0:T(8,128)(2,1)S(1)} all-gather(bf16[1,64,768]{2,1,0:T(8,128)(2,1)S(1)} %fusion.55), channel_id=1, replica_groups=mesh['section'=2,'row'=32,'col'=4] {'col'}, dimensions={2}, use_global_device_ids=true | all-gather | bytes 491520 | tf_op jit(solution)/shard_map/all_gather | solution.py:81
  69.3 141.3 %all-gather.2.cloned.1.call-done = bf16[1,3072,3,768]{3,1,2,0:T(8,128)(2,1)} async-done(((bf16[1,96,3,768]{3,1,2,0:T(8,128)(2,1)}), bf16[1,3072,3,768]{3,1,2,0:T(8,128)(2,1)}) %all-gather.2.cloned.1.call-update) | async-done | bytes 14155792 | tf_op jit(solution)/shard_map/all_gather | solution.py:91
  210.6 18.6 %copy.139 = bf16[1,3072,3,768]{1,3,2,0:T(8,128)(2,1)} copy(bf16[1,3072,3,768]{3,1,2,0:T(8,128)(2,1)} %all-gather.2.cloned.1.call-done) | data formatting | bytes 28311552 | tf_op jit(solution)/shard_map/all_gather | solution.py:91
  229.2 9.4 %fusion.17 = f32[1,64,3,768]{3,1,2,0:T(8,128)S(1)} fusion(bf16[1,3072,3,768]{1,3,2,0:T(8,128)(2,1)} %copy.139, bf16[1,64,3072]{2,1,0:T(8,128)(2,1)S(1)} %all_gather.18), kind=kOutput, calls=%fused_computation.22 | convolution fusion | flops 905969664 | bytes 15138816 | tf_op jit(solution)/shard_map/dot_general | solution.py:124
  242.7 1.5 scatter.50
  244.5 1.5 scatter.51
  246.9 4.6 fusion.12
  253.5 3.1 and_reduce_fusion.2
  256.6 17.3 %reduce-scatter.6.cloned.1.call-done = bf16[1,64,768]{2,1,0:T(8,128)(2,1)} async-done(((bf16[1,64,3072]{2,1,0:T(8,128)(2,1)}), bf16[1,64,768]{2,1,0:T(8,128)(2,1)}) %reduce-scatter.6.cloned.1.call-update) | async-done | bytes 98320 | tf_op jit(solution)/shard_map/reduce_scatter | solution.py:138
  273.9 1.6 select_select_fusion
  277.9 8.6 %all-reduce.6 = (f32[1,64]{1,0:T(1,128)S(1)}, f32[1,64]{1,0:T(1,128)S(1)}) all-reduce(f32[1,64]{1,0:T(1,128)S(1)} %bitcast.438, f32[1,64]{1,0:T(1,128)S(1)} %bitcast.437), channel_id=1, replica_groups=mesh['section'=2,'row'=32,'col'=4] {'col'}, use_global_device_ids=true, to_apply=%region_13.14 | all-reduce | flops 128 | bytes 1024 | tf_op jit(solution)/shard_map/psum | solution.py:70
  286.7 12.9 %all_gather.20 = bf16[1,64,3072]{2,1,0:T(8,128)(2,1)S(1)} all-gather(bf16[1,64,768]{2,1,0:T(8,128)(2,1)S(1)} %fusion.62), channel_id=1, replica_groups=mesh['section'=2,'row'=32,'col'=4] {'col'}, dimensions={2}, use_global_device_ids=true | all-gather | bytes 491520 | tf_op jit(solution)/shard_map/all_gather | solution.py:81
  299.5 9.4 %fusion.20 = f32[1,64,3,768]{3,1,2,0:T(8,128)S(1)} fusion(bf16[1,3072,3,768]{1,3,2,0:T(8,128)(2,1)} %copy.139, bf16[1,64,3072]{2,1,0:T(8,128)(2,1)S(1)} %all_gather.20), kind=kOutput, calls=%fused_computation.23 | convolution fusion | flops 905969664 | bytes 15138816 | tf_op jit(solution)/shard_map/dot_general | solution.py:124
  315.3 4.6 fusion.13
  320.8 1.5 scatter.54
  322.3 21.0 %reduce-scatter.8.cloned.1.call-done = bf16[1,64,768]{2,1,0:T(8,128)(2,1)} async-done(((bf16[1,64,3072]{2,1,0:T(8,128)(2,1)}), bf16[1,64,768]{2,1,0:T(8,128)(2,1)}) %reduce-scatter.8.cloned.1.call-update) | async-done | bytes 98320 | tf_op jit(solution)/shard_map/reduce_scatter | solution.py:138
  343.3 2.2 fusion.151
  347.8 8.6 %all-reduce.5 = (f32[1,64]{1,0:T(1,128)S(1)}, f32[1,64]{1,0:T(1,128)S(1)}) all-reduce(f32[1,64]{1,0:T(1,128)S(1)} %bitcast.440, f32[1,64]{1,0:T(1,128)S(1)} %bitcast.439), channel_id=1, replica_groups=mesh['section'=2,'row'=32,'col'=4] {'col'}, use_global_device_ids=true, to_apply=%region_22.23 | all-reduce | flops 128 | bytes 1024 | tf_op jit(solution)/shard_map/psum | solution.py:70
  356.6 12.7 %all_gather.21 = bf16[1,64,3072]{2,1,0:T(8,128)(2,1)S(1)} all-gather(bf16[1,64,768]{2,1,0:T(8,128)(2,1)S(1)} %fusion.69), channel_id=1, replica_groups=mesh['section'=2,'row'=32,'col'=4] {'col'}, dimensions={2}, use_global_device_ids=true | all-gather | bytes 491520 | tf_op jit(solution)/shard_map/all_gather | solution.py:81
  369.2 9.4 %fusion.23 = f32[1,64,3,768]{3,1,2,0:T(8,128)S(1)} fusion(bf16[1,3072,3,768]{1,3,2,0:T(8,128)(2,1)} %copy.139, bf16[1,64,3072]{2,1,0:T(8,128)(2,1)S(1)} %all_gather.21), kind=kOutput, calls=%fused_computation.24 | convolution fusion | flops 905969664 | bytes 15138816 | tf_op jit(solution)/shard_map/dot_general | solution.py:124
  379.6 2.1 fusion.107
  381.8 1.5 scatter.61
  383.3 1.5 scatter.60
  386.1 4.6 fusion.14
  392.9 21.1 %reduce-scatter.10.cloned.1.call-done = bf16[1,64,768]{2,1,0:T(8,128)(2,1)} async-done(((bf16[1,64,3072]{2,1,0:T(8,128)(2,1)}), bf16[1,64,768]{2,1,0:T(8,128)(2,1)}) %reduce-scatter.10.cloned.1.call-update) | async-done | bytes 98320 | tf_op jit(solution)/shard_map/reduce_scatter | solution.py:138
  414.0 2.3 fusion.150
  416.4 1.5 collective-permute-start.2
  418.8 8.6 %all-reduce.4 = (f32[1,64]{1,0:T(1,128)S(1)}, f32[1,64]{1,0:T(1,128)S(1)}) all-reduce(f32[1,64]{1,0:T(1,128)S(1)} %bitcast.442, f32[1,64]{1,0:T(1,128)S(1)} %bitcast.441), channel_id=1, replica_groups=mesh['section'=2,'row'=32,'col'=4] {'col'}, use_global_device_ids=true, to_apply=%region_31.32 | all-reduce | flops 128 | bytes 1024 | tf_op jit(solution)/shard_map/psum | solution.py:70
  427.5 12.7 %all_gather.22 = bf16[1,64,3072]{2,1,0:T(8,128)(2,1)S(1)} all-gather(bf16[1,64,768]{2,1,0:T(8,128)(2,1)S(1)} %fusion.76), channel_id=1, replica_groups=mesh['section'=2,'row'=32,'col'=4] {'col'}, dimensions={2}, use_global_device_ids=true | all-gather | bytes 491520 | tf_op jit(solution)/shard_map/all_gather | solution.py:81
  440.2 9.4 %fusion.26 = f32[1,64,3,768]{3,1,2,0:T(8,128)S(1)} fusion(bf16[1,3072,3,768]{1,3,2,0:T(8,128)(2,1)} %copy.139, bf16[1,64,3072]{2,1,0:T(8,128)(2,1)S(1)} %all_gather.22), kind=kOutput, calls=%fused_computation.25 | convolution fusion | flops 905969664 | bytes 15138816 | tf_op jit(solution)/shard_map/dot_general | solution.py:124
  450.6 2.1 fusion.109
  456.9 4.6 fusion.15
  462.2 1.5 scatter.64
  463.7 21.0 %reduce-scatter.12.cloned.1.call-done = bf16[1,64,768]{2,1,0:T(8,128)(2,1)} async-done(((bf16[1,64,3072]{2,1,0:T(8,128)(2,1)}), bf16[1,64,768]{2,1,0:T(8,128)(2,1)}) %reduce-scatter.12.cloned.1.call-update) | async-done | bytes 98320 | tf_op jit(solution)/shard_map/reduce_scatter | solution.py:138
  484.8 2.3 fusion.149
  489.4 8.6 %all-reduce.3 = (f32[1,64]{1,0:T(1,128)S(1)}, f32[1,64]{1,0:T(1,128)S(1)}) all-reduce(f32[1,64]{1,0:T(1,128)S(1)} %bitcast.436, f32[1,64]{1,0:T(1,128)S(1)} %bitcast.435), channel_id=1, replica_groups=mesh['section'=2,'row'=32,'col'=4] {'col'}, use_global_device_ids=true, to_apply=%region_40.41 | all-reduce | flops 128 | bytes 1024 | tf_op jit(solution)/shard_map/psum | solution.py:70
  498.2 12.9 %all_gather.23 = bf16[1,64,3072]{2,1,0:T(8,128)(2,1)S(1)} all-gather(bf16[1,64,768]{2,1,0:T(8,128)(2,1)S(1)} %fusion.83), channel_id=1, replica_groups=mesh['section'=2,'row'=32,'col'=4] {'col'}, dimensions={2}, use_global_device_ids=true | all-gather | bytes 491520 | tf_op jit(solution)/shard_map/all_gather | solution.py:81
  511.1 9.4 %fusion.29 = f32[1,64,3,768]{3,1,2,0:T(8,128)S(1)} fusion(bf16[1,3072,3,768]{1,3,2,0:T(8,128)(2,1)} %copy.139, bf16[1,64,3072]{2,1,0:T(8,128)(2,1)S(1)} %all_gather.23), kind=kOutput, calls=%fused_computation.26 | convolution fusion | flops 905969664 | bytes 15138816 | tf_op jit(solution)/shard_map/dot_general | solution.py:124
  527.1 4.6 fusion.16
  531.8 1.5 scatter.69
  533.3 21.8 %reduce-scatter.14.cloned.1.call-done = bf16[1,64,768]{2,1,0:T(8,128)(2,1)} async-done(((bf16[1,64,3072]{2,1,0:T(8,128)(2,1)}), bf16[1,64,768]{2,1,0:T(8,128)(2,1)}) %reduce-scatter.14.cloned.1.call-update) | async-done | bytes 98320 | tf_op jit(solution)/shard_map/reduce_scatter | solution.py:138
  555.0 2.3 fusion.128
  (208 shorter events, 43.5 us)
Async XLA Ops:
  6.5 204.1 %all-gather.2.cloned.1.call-start = ((), (), s32[]{:S(2)}) async-start(), calls=%async_computation.6 | async-start | bytes 14598144 | tf_op jit(solution)/shard_map/all_gather | solution.py:91
  10.9 12.0 %copy-start.3 = (s32[1,4]{1,0:T(1,128)S(1)}, s32[1,4]{1,0:T(1,128)}, u32[]{:S(2)}) copy-start(s32[1,4]{1,0:T(1,128)} %param.39) | copy-start | bytes 52
  10.9 17.4 %copy-start.2 = (bf16[1,1,256,768]{3,2,1,0:T(8,128)(2,1)S(1)}, bf16[1,1,256,768]{3,2,1,0:T(8,128)(2,1)}, u32[]{:S(2)}) copy-start(bf16[1,1,256,768]{3,2,1,0:T(8,128)(2,1)} %param.44) | copy-start | bytes 1179652
  10.9 17.4 %copy-start.1 = (bf16[1,1,256,768]{3,2,1,0:T(8,128)(2,1)S(1)}, bf16[1,1,256,768]{3,2,1,0:T(8,128)(2,1)}, u32[]{:S(2)}) copy-start(bf16[1,1,256,768]{3,2,1,0:T(8,128)(2,1)} %param.45) | copy-start | bytes 1179652
  10.9 236.0 %all-to-all-start = ((bf16[32,1,768,96]{2,3,1,0:T(8,128)(2,1)}), bf16[32,1,768,96]{2,3,1,0:T(8,128)(2,1)}, u32[]{:S(2)}, u32[]{:S(2)}) async-start(bf16[32,1,768,96]{2,3,1,0:T(8,128)(2,1)} %stack.2), calls=%async_computation | async-start | bytes 9437184 | tf_op jit(solution)/shard_map/all_to_all | solution.py:93
  22.8 251.1 %reduce-scatter.6.cloned.1.call-start = ((), (), s32[]{:S(2)}) async-start(), calls=%async_computation.7 | async-start | bytes 491520 | tf_op jit(solution)/shard_map/reduce_scatter | solution.py:138
  28.4 6.7 %copy-start = (bf16[1,256,768]{2,1,0:T(8,128)(2,1)S(1)}, bf16[1,256,768]{2,1,0:T(8,128)(2,1)}, u32[]{:S(2)}) copy-start(bf16[1,256,768]{2,1,0:T(8,128)(2,1)} %param.38) | copy-start | bytes 1179652
  35.1 15.1 %copy-start.4 = (s32[1,2]{1,0:T(1,128)S(1)}, s32[1,2]{1,0:T(1,128)}, u32[]{:S(2)}) copy-start(s32[1,2]{1,0:T(1,128)} %constant.478.clone.1) | copy-start | bytes 28
  35.1 17.0 %copy-start.5 = (s32[3]{0:T(128)S(1)}, s32[3]{0:T(128)}, u32[]{:S(2)}) copy-start(s32[3]{0:T(128)} %constant.479.clone.1) | copy-start | bytes 40
  251.6 91.7 %reduce-scatter.8.cloned.1.call-start = ((), (), s32[]{:S(2)}) async-start(), calls=%async_computation.8 | async-start | bytes 491520 | tf_op jit(solution)/shard_map/reduce_scatter | solution.py:138
  275.6 2.2 collective-permute-start
  320.0 94.1 %reduce-scatter.10.cloned.1.call-start = ((), (), s32[]{:S(2)}) async-start(), calls=%async_computation.9 | async-start | bytes 491520 | tf_op jit(solution)/shard_map/reduce_scatter | solution.py:138
  345.4 2.2 collective-permute-start.1
  385.5 28.6 %copy-start.7 = (pred[64]{0:T(512)(128)(4,1)S(1)}, pred[64]{0:T(512)(128)(4,1)}, u32[]{:S(2)}) copy-start(pred[64]{0:T(512)(128)(4,1)} %broadcast_and_fusion.2) | copy-start | bytes 196
  390.7 94.0 %reduce-scatter.12.cloned.1.call-start = ((), (), s32[]{:S(2)}) async-start(), calls=%async_computation.10 | async-start | bytes 491520 | tf_op jit(solution)/shard_map/reduce_scatter | solution.py:138
  416.4 2.2 collective-permute-start.2
  456.2 28.5 %copy-start.6 = (pred[64]{0:T(512)(128)(4,1)S(1)}, pred[64]{0:T(512)(128)(4,1)}, u32[]{:S(2)}) copy-start(pred[64]{0:T(512)(128)(4,1)} %broadcast_and_fusion.1) | copy-start | bytes 196
  461.5 93.6 %reduce-scatter.14.cloned.1.call-start = ((), (), s32[]{:S(2)}) async-start(), calls=%async_computation.11 | async-start | bytes 491520 | tf_op jit(solution)/shard_map/reduce_scatter | solution.py:138
  487.0 2.2 collective-permute-start.3
Sparse Core Ops, SparseCore 0:
  9.9 200.6 all-gather.1
  251.7 22.2 reduce-scatter.5
  320.1 23.1 reduce-scatter.7
  390.8 23.1 reduce-scatter.9
  461.6 23.0 reduce-scatter.11
  531.9 23.1 reduce-scatter.13
